TPU v7x, 32 devices: a whole 2x2x4 slice. The times are simulated.
32 devices in a mesh: gx: 8 (over y, x, core), gy: 4 (over z).
Axes of the slice: x: 2, y: 2, z: 4, core: 2. Of those that a mesh axis runs over, the one named last changes fastest.
Arguments:
- coefficient: float32 [2, 2, 2, 64, 64, 128], P(None, None, None, 'gx', 'gy'), may hold values from 0.05 to 5
- owner: int32 [64, 64], P('gx', 'gy'), may hold values from 0 to 31, as said below
- w_in: bfloat16 [128, 27], replicated, may hold values from -1.25 to 1.25
- b_in: float32 [128], replicated, may hold values from -3 to 3
- w_mid: bfloat16 [2, 128, 128], replicated, may hold values from -0.5 to 0.5
- b_mid: float32 [2, 128], replicated, may hold values from -3 to 3
- w_out: bfloat16 [27, 128], replicated, may hold values from -0.5 to 0.5
- b_out: float32 [27], replicated, may hold values from -4 to 4
Outputs:
- relaid: float32 [8192, 27, 128], P(('gx', 'gy'))
Inputs may be any that keep to these rules, and one draw needn't show every extreme that they name: Among the 8 x 16 columns of one device, no owner appears more than 8 times, and one owner, the same for every device, appears exactly 8 times on every device.
All inputs are finite; a program needn't handle non-finite values.
Results may differ from a plain program's by a relative error of at most 0.004.
Values sent between devices are 32-bit elements; how exact they have to be, the bound alone decides.
A program may use at most 128 MiB of HBM per device.

v0:
```python
import functools

import jax
import jax.numpy as jnp
import numpy as np
from jax import lax
from jax.experimental import pallas as pl
from jax.experimental.pallas import tpu as pltpu
from jax.sharding import PartitionSpec as P

CORNERS = [(a, b, c) for a in (0, 1) for b in (0, 1) for c in (0, 1)]
OFFSETS = [(a, b, c) for a in (-1, 0, 1) for b in (-1, 0, 1) for c in (-1, 0, 1)]
PAIRS = [(s, t) for s in range(8) for t in range(s, 8)]
PAIR_ROW = {pair: row for row, pair in enumerate(PAIRS)}
POINT_ROWS = 64
FACE_ROWS = 16


def corner_row(corner):
    return corner[0] * 4 + corner[1] * 2 + corner[2]


def point_row(offset):
    return (offset[0] + 1) * 9 + (offset[1] + 1) * 3 + offset[2] + 1


def pair_row(first, second):
    low, high = sorted((corner_row(first), corner_row(second)))
    return PAIR_ROW[low, high]


def edge_form(weight, root, store):
    def value(node, delta):
        offset = tuple(n - 2 * d for n, d in zip(node, delta))
        if min(offset) < -1 or max(offset) > 1:
            return None
        return weight(offset, delta)

    total = {}
    for direction in range(3):
        for node in CORNERS:
            other = tuple(n + (axis == direction) for axis, n in enumerate(node))
            face = root(node) * root(other)
            drops = []
            for delta in CORNERS:
                here, there = value(node, delta), value(other, delta)
                if here is None and there is None:
                    continue
                if there is None:
                    drops.append((delta, here))
                elif here is None:
                    drops.append((delta, -there))
                else:
                    drops.append((delta, here - there))
            for index, (first, drop) in enumerate(drops):
                scaled = face * drop
                for second, other_drop in drops[index:]:
                    row = pair_row(first, second)
                    term = scaled * other_drop
                    total[row] = total[row] + term if row in total else term
    for row, entry in total.items():
        store(row, entry)


def compute_kernel(
    flags, *rest,
):
    far, rest = rest[:12], rest[12:]
    blocks, kbuf, logs, roots, wbuf, pairs, w_first, w_half, biases = rest[:9]
    near, row_sems = rest[9:21], rest[21]
    own, low_x, high_x, low_y, high_y, pick, w_in, w_mid, w_out, b_in, b_mid, b_out = near
    fetches = [
        pltpu.make_async_copy(source, target, row_sems.at[number])
        for number, (source, target) in enumerate(zip(far, near))
    ]
    for fetch in fetches:
        fetch.start()

    _, cx, cy, cz = own.shape
    nx, ny = cx + 4, cy + 4
    wide = cy + 2
    columns = cx * cy
    layers = w_mid.shape[0]

    for fetch in fetches[:5]:
        fetch.wait()
    for p in range(8):
        for x in range(nx):
            start = x * ny * 8 + p
            middle = low_x[p, x] if x < 2 else high_x[p, x - 2 - cx] if x >= cx + 2 else own[p, x - 2]
            kbuf[pl.ds(start + 16, cy, stride=8), :] = middle
            kbuf[pl.ds(start, 2, stride=8), :] = low_y[p, x]
            kbuf[pl.ds(start + (cy + 2) * 8, 2, stride=8), :] = high_y[p, x]

    lane = lax.broadcasted_iota(jnp.int32, (8, cz), 1)

    @pl.loop(0, nx)
    def _(x):
        for y in range(ny):
            kappa = kbuf[pl.ds(pl.multiple_of((x * ny + y) * 8, 8), 8), :]
            value = jnp.log1p(kappa)
            below = jnp.where(lane == 0, 0.0, pltpu.roll(value, 1, 1))
            logs[x * ny + y] = jnp.concatenate([value, below], axis=0).astype(jnp.bfloat16)

    @pl.loop(1, nx - 1)
    def _(x):
        for y in range(1, ny - 1):
            root = jnp.sqrt(kbuf[pl.ds(pl.multiple_of((x * ny + y) * 8, 8), 8), :])
            above = jnp.where(lane == cz - 1, 0.0, pltpu.roll(root, cz - 1, 1))
            row = pl.multiple_of(((x - 1) * wide + y - 1) * FACE_ROWS, FACE_ROWS)
            roots[pl.ds(row, 8), :] = root
            roots[pl.ds(row + 8, 8), :] = above

    for fetch in fetches[5:]:
        fetch.wait()
    w_first[...] = (0.5 * jnp.dot(w_in[...], pick[...], preferred_element_type=jnp.float32)).astype(
        jnp.bfloat16
    )
    for m in range(layers):
        w_half[m] = w_mid[m] * jnp.bfloat16(0.5)
    w_half[layers] = jnp.zeros(w_half.shape[1:], jnp.bfloat16)
    w_half[layers, :27] = w_out[...] * jnp.bfloat16(0.5)
    for m in range(layers + 2):
        bias = b_in[...] if m == 0 else b_out[...] if m > layers else b_mid[m - 1:m, :]
        biases[m] = jnp.transpose(jnp.broadcast_to(0.5 * bias, biases.shape[1:]))

    group = max(g for g in range(1, 7) if wide % g == 0)
    lane_out = lax.broadcasted_iota(jnp.int32, (32, cz), 1)

    def activate(value):
        return (value + value * jnp.tanh(value)).astype(jnp.bfloat16)

    def biased(value, m):
        bias = biases[m, :value.shape[0], :]
        return value + jnp.concatenate([bias] * group, axis=1)

    @pl.loop(0, (cx + 2) * (wide // group))
    def _(step):
        x = step // (wide // group) + 1
        y = step % (wide // group) * group + 1
        parts = []
        for k in range(group):
            at = x * ny + y + k
            parts.append(
                jnp.concatenate([logs[at], logs[at - ny], logs[at - 1], logs[at - ny - 1]], axis=0)
            )
        rows = jnp.concatenate(parts, axis=1)
        hidden = activate(biased(jnp.dot(w_first[...], rows, preferred_element_type=jnp.float32), 0))
        for m in range(layers):
            hidden = activate(
                biased(jnp.dot(w_half[m], hidden, preferred_element_type=jnp.float32), m + 1)
            )
        last = jnp.dot(w_half[layers, :32], hidden, preferred_element_type=jnp.float32)
        weights = 0.25 + 0.25 * jnp.tanh(biased(last, layers + 1))
        for k in range(group):
            outside = (
                ((x == 1) & (flags[0] == 0))
                | ((x == cx + 2) & (flags[1] == 0))
                | ((y + k == 1) & (flags[2] == 0))
                | ((y + k == cy + 2) & (flags[3] == 0))
            )
            keep = jnp.where(outside, 0.0, 1.0)
            column = weights[:, k * cz:(k + 1) * cz] * keep
            above = jnp.where(lane_out == cz - 1, 0.0, pltpu.roll(column, cz - 1, 1))
            row = pl.multiple_of(((x - 1) * wide + y + k - 1) * POINT_ROWS, POINT_ROWS)
            wbuf[pl.ds(row, 32), :] = column
            wbuf[pl.ds(row + 32, 32), :] = above

    @pl.loop(0, pl.cdiv((cx + 1) * wide, 8))
    def _(tile):
        base = tile * 8

        def weight(offset, delta):
            column = base + delta[0] * wide + delta[1]
            row = point_row(offset) + 32 * delta[2]
            return wbuf[pl.ds(column * POINT_ROWS + row, 8, stride=POINT_ROWS), :]

        def root(node):
            column = base + node[0] // 2 * wide + node[1] // 2
            row = corner_row(tuple(n % 2 for n in node)) + 8 * (node[2] // 2)
            return roots[pl.ds(column * FACE_ROWS + row, 8, stride=FACE_ROWS), :]

        def store(row, entry):
            pairs[pl.ds(base * len(PAIRS) + row, 8, stride=len(PAIRS)), :] = entry

        edge_form(weight, root, store)

    blocks[pl.ds(columns * 32, 32), :] = jnp.zeros((32, cz), jnp.float32)

    @pl.loop(0, cx * (cy // 8))
    def _(tile):
        x = tile // (cy // 8)
        y = tile % (cy // 8) * 8
        cell = (x + 1) * wide + y + 1
        for number, offset in enumerate(OFFSETS):
            sums = [None, None]
            for first in CORNERS:
                second = tuple(f + o for f, o in zip(first, offset))
                if min(second) < 0 or max(second) > 1:
                    continue
                base = cell - first[0] * wide - first[1]
                start = base * len(PAIRS) + pair_row(first, second)
                entry = pairs[pl.ds(start, 8, stride=len(PAIRS)), :]
                seen = sums[first[2]]
                sums[first[2]] = entry if seen is None else seen + entry
            if sums[1] is not None:
                moved = pltpu.roll(sums[1], 1, 1)
                sums[0] = moved if sums[0] is None else sums[0] + moved
            blocks[pl.ds((x * cy + y) * 32 + number, 8, stride=32), :] = sums[0]


def hand_kernel(n_gx, n_gy, source, blocks, out, held, send_sems, recv_sems, own_sem):
    devices = n_gx * n_gy
    by_point = out.shape[0] == 27
    most = out.shape[1 if by_point else 0] // devices
    ix, iy = lax.axis_index("gx"), lax.axis_index("gy")
    me = ix * n_gy + iy
    half = n_gy // 2

    def partner(k):
        far = k // (devices // 2)
        side = (iy // half + 1 + far) % 2
        step = k % (devices // 2)
        return (ix + step % n_gx) % n_gx, side * half + (iy + step // n_gx) % half

    barrier = pltpu.get_barrier_semaphore()

    def each(action):
        pl.loop(0, devices // 2)(action)
        pl.loop(devices // 2 + 1, devices)(action)

    @each
    def _(k):
        px, py = partner(k)
        pl.semaphore_signal(
            barrier, inc=1, device_id=(px, py), device_id_type=pl.DeviceIdType.MESH
        )

    @pl.loop(0, devices)
    def _(device):
        for rank in range(most):
            slot = device * most + rank
            block = blocks[source[slot], :27, :]
            if by_point:
                held[:, slot, :] = block
            else:
                held[slot] = block

    pl.semaphore_wait(barrier, devices - 1)

    def slots_of(ref, device):
        if by_point:
            return ref.at[:, pl.ds(pl.multiple_of(device * most, 8), most)]
        return ref.at[pl.ds(device * most, most)]

    def copy(k, home):
        px, py = partner(k)
        other = px * n_gy + py
        return pltpu.make_async_remote_copy(
            src_ref=slots_of(held, other),
            dst_ref=slots_of(out, home),
            send_sem=send_sems.at[other],
            recv_sem=recv_sems.at[home],
            device_id=(px, py),
            device_id_type=pl.DeviceIdType.MESH,
        )

    @each
    def _(k):
        copy(k, me).start()

    mine = pltpu.make_async_copy(
        slots_of(held, me), slots_of(out, me), own_sem
    )
    mine.start()

    @each
    def _(k):
        px, py = partner(k)
        copy(k, me).wait_send()
        copy(k, px * n_gy + py).wait_recv()

    mine.wait()


def halo_kernel(n_gx, n_gy, own, low_x, high_x, low_y, high_y, edges, send_sems, recv_sems):
    _, cx, cy, _ = own.shape
    ix, iy = lax.axis_index("gx"), lax.axis_index("gy")
    mesh_id = pl.DeviceIdType.MESH
    ways = [(a, b) for a in (-1, 0, 1) for b in (-1, 0, 1) if a or b]

    def exists(way):
        x, y = ix + way[0], iy + way[1]
        return (x >= 0) & (x < n_gx) & (y >= 0) & (y < n_gy)

    def landing(way):
        if way[1] == 0:
            return low_x if way[0] < 0 else high_x
        rim = low_y if way[1] < 0 else high_y
        start = (0, 2, cx + 2)[way[0] + 1]
        return rim.at[:, pl.ds(start, cx if way[0] == 0 else 2)]

    def leaving(way):
        if way[1] == 0:
            return own.at[:, pl.ds(0 if way[0] < 0 else cx - 2, 2)]
        rim = edges.at[0 if way[1] < 0 else 1]
        return rim.at[:, pl.ds(cx - 2 if way[0] > 0 else 0, cx if way[0] == 0 else 2)]

    barrier = pltpu.get_barrier_semaphore()
    for way in ways:
        @pl.when(exists(way))
        def _(way=way):
            pl.semaphore_signal(
                barrier, inc=1, device_id=(ix + way[0], iy + way[1]), device_id_type=mesh_id
            )

    edges[0] = own[:, :, :2, :]
    edges[1] = own[:, :, cy - 2:, :]
    for way in ways:
        @pl.when(jnp.logical_not(exists(way)))
        def _(way=way):
            part = landing(way)
            part[...] = jnp.zeros(part.shape, jnp.float32)

    rows = 1 + (ix > 0).astype(jnp.int32) + (ix < n_gx - 1).astype(jnp.int32)
    lines = 1 + (iy > 0).astype(jnp.int32) + (iy < n_gy - 1).astype(jnp.int32)
    pl.semaphore_wait(barrier, rows * lines - 1)

    def copy(number, way):
        back = (-way[0], -way[1])
        return pltpu.make_async_remote_copy(
            src_ref=leaving(way),
            dst_ref=landing(back),
            send_sem=send_sems.at[number],
            recv_sem=recv_sems.at[number],
            device_id=(ix + way[0], iy + way[1]),
            device_id_type=mesh_id,
        )

    for number, way in enumerate(ways):
        @pl.when(exists(way))
        def _(number=number, way=way):
            copy(number, way).start()

    for number, way in enumerate(ways):
        @pl.when(exists(way))
        def _(number=number, way=way):
            copy(number, way).wait_send()

        @pl.when(exists((-way[0], -way[1])))
        def _(number=number, way=way):
            copy(number, way).wait_recv()


def per_device(coefficient, owner, w_in, b_in, w_mid, b_mid, w_out, b_out):
    cx, cy, cz = coefficient.shape[3:]
    hid = w_in.shape[0]
    own = coefficient.reshape(8, cx, cy, cz)
    size = lax.axis_size("gy")
    vmem = pl.BlockSpec(memory_space=pltpu.VMEM)
    smem = pl.BlockSpec(memory_space=pltpu.SMEM)
    rim_x = jax.ShapeDtypeStruct((8, 2, cy, cz), jnp.float32)
    rim_y = jax.ShapeDtypeStruct((8, cx + 4, 2, cz), jnp.float32)
    low_x, high_x, low_y, high_y = pl.pallas_call(
        functools.partial(halo_kernel, lax.axis_size("gx"), size),
        out_shape=(rim_x, rim_x, rim_y, rim_y),
        in_specs=[vmem],
        out_specs=(vmem, vmem, vmem, vmem),
        scratch_shapes=[
            pltpu.VMEM((2, 8, cx, 2, cz), jnp.float32),
            pltpu.SemaphoreType.DMA((8,)),
            pltpu.SemaphoreType.DMA((8,)),
        ],
        compiler_params=pltpu.CompilerParams(collective_id=1, has_side_effects=True),
        name="halo",
    )(own)

    devices = lax.axis_size("gx") * lax.axis_size("gy")
    columns = cx * cy
    most = 2 * columns // devices
    owners = owner.reshape(-1)
    place = jnp.arange(columns, dtype=jnp.int32)
    same = (owners[:, None] == owners[None, :]) & (place[None, :] < place[:, None])
    rank = jnp.sum(same.astype(jnp.int32), axis=1)
    slot = owners * most + rank
    hits = slot[None, :] == jnp.arange(devices * most, dtype=jnp.int32)[:, None]
    source = columns + jnp.sum(jnp.where(hits, place[None, :] - columns, 0), axis=1)

    ix, iy = lax.axis_index("gx"), lax.axis_index("gy")
    flags = jnp.stack(
        [ix > 0, ix < lax.axis_size("gx") - 1, iy > 0, iy < size - 1]
    ).astype(jnp.int32)

    pick = np.zeros((27, 64), np.float32)
    row = 0
    for dx, dy in ((0, 0), (1, 0), (0, 1), (1, 1)):
        for dz in (0, 1):
            for corner in CORNERS:
                shift = (dx, dy, dz)
                if all(s <= c for s, c in zip(shift, corner)):
                    pick[point_row(tuple(c - 2 * s for s, c in zip(shift, corner))), row] = 1.0
                row += 1

    wide = cy + 2
    tiles = -(-((cx + 1) * wide) // 8) * 8
    held = max((cx + 2) * wide, tiles + wide + 2)
    small = (
        own, low_x, high_x, low_y, high_y,
        jnp.asarray(pick, jnp.bfloat16), w_in, w_mid, w_out,
        b_in[None, :], b_mid, jnp.pad(b_out, (0, hid - 27))[None, :],
    )
    blocks = pl.pallas_call(
        compute_kernel,
        out_shape=jax.ShapeDtypeStruct(((columns + 1) * 32, cz), jnp.float32),
        in_specs=[smem] + [pl.BlockSpec(memory_space=pltpu.HBM)] * len(small),
        out_specs=vmem,
        scratch_shapes=[
            pltpu.VMEM(((cx + 4) * (cy + 4) * 8 + 8, cz), jnp.float32),
            pltpu.VMEM(((cx + 4) * (cy + 4), 16, cz), jnp.bfloat16),
            pltpu.VMEM((held * FACE_ROWS, cz), jnp.float32),
            pltpu.VMEM((held * POINT_ROWS, cz), jnp.float32),
            pltpu.VMEM(((tiles + 1) * len(PAIRS), cz), jnp.float32),
            pltpu.VMEM((hid, 64), jnp.bfloat16),
            pltpu.VMEM((w_mid.shape[0] + 1, hid, hid), jnp.bfloat16),
            pltpu.VMEM((w_mid.shape[0] + 2, hid, cz), jnp.float32),
            *[pltpu.VMEM(part.shape, part.dtype) for part in small],
            pltpu.SemaphoreType.DMA((len(small),)),
        ],
        compiler_params=pltpu.CompilerParams(vmem_limit_bytes=67043328),
        name="stencil",
    )(
        flags, *small,
    )
    slots = devices * most
    by_point = most % 8 == 0
    shape = (27, slots, cz) if by_point else (slots, 27, cz)
    relaid = pl.pallas_call(
        functools.partial(hand_kernel, lax.axis_size("gx"), size),
        out_shape=jax.ShapeDtypeStruct(shape, jnp.float32),
        in_specs=[smem, vmem],
        out_specs=pl.BlockSpec(memory_space=pl.ANY),
        scratch_shapes=[
            pltpu.VMEM(shape, jnp.float32),
            pltpu.SemaphoreType.DMA((devices,)),
            pltpu.SemaphoreType.DMA((devices,)),
            pltpu.SemaphoreType.DMA,
        ],
        compiler_params=pltpu.CompilerParams(
            collective_id=0, has_side_effects=True, vmem_limit_bytes=24 << 20
        ),
        name="hand",
    )(source, blocks.reshape(columns + 1, 32, cz))
    return jnp.transpose(relaid, (1, 0, 2)) if by_point else relaid


def solution(mesh):
    return jax.shard_map(
        per_device,
        mesh=mesh,
        in_specs=(
            P(None, None, None, "gx", "gy", None),
            P("gx", "gy"),
            P(),
            P(),
            P(),
            P(),
            P(),
            P(),
        ),
        out_specs=P(("gx", "gy"), None, None),
        check_vma=False,
    )
```

profile of v0, /device:TPU:8, one launch (start us, length us, event | category | flops | bytes accessed | tf_op | source)
XLA Modules:
  0.0 138.0 jit_solution(2295620198770254319)
XLA Ops:
  0.0 0.6 add_convert_fusion.flags
  0.6 0.8 reshape.24
  1.4 0.2 convert_reduce_fusion
  1.6 0.1 select_reduce_fusion
  1.7 0.6 broadcast_add_fusion.source
  2.3 1.2 pad_bitcast_fusion.rest_11_
  3.5 1.4 %copy.11.rest_6_ = bf16[128,27]{1,0:T(8,128)(2,1)} copy(bf16[128,27]{0,1:T(8,128)(2,1)} %param.11) | data formatting | bytes 13824 | tf_op args[2]
  4.9 7.7 %halo.1 = (f32[8,2,16,128]{3,2,1,0:T(8,128)}, f32[8,2,16,128]{3,2,1,0:T(8,128)}, f32[8,12,2,128]{3,2,1,0:T(2,128)}, f32[8,12,2,128]{3,2,1,0:T(2,128)}) custom-call(f32[8,8,16,128]{3,2,1,0:T(8,128)} %bitcast.12), custom_call_target="tpu_custom_call" | custom-call | tf_op jit(solution)/shard_map/halo/pallas_call | solution.py:364
  12.6 35.1 %stencil.1 = f32[4128,128]{1,0:T(8,128)} custom-call(s32[4]{0:T(128)} %add_convert_fusion.flags, f32[8,8,16,128]{3,2,1,0:T(8,128)} %bitcast.13, f32[8,2,16,128]{3,2,1,0:T(8,128)} %get-tuple-element.9.rest_1_, f32[8,2,16,128]{3,2,1,0:T(8,128)} %get-tuple-element.10.rest_2_, f32[8,12,2,128]{3,2,1,0:T(2,128)} %get-tuple-element.11.rest_3_, ...), custom_call_target="tpu_custom_call" | custom-call | tf_op jit(solution)/shard_map/stencil/pallas_call | solution.py:412
  47.7 0.0 copy-start
  47.8 1.6 %copy-done = f32[4128,128]{1,0:T(8,128)S(1)} copy-done((f32[4128,128]{1,0:T(8,128)S(1)}, f32[4128,128]{1,0:T(8,128)}, u32[]{:S(2)}) %copy-start) | copy-done | bytes 2113560
  49.3 0.0 copy-start.1
  49.3 0.7 copy-done.1
  50.0 86.2 %hand.1 = f32[27,256,128]{2,1,0:T(8,128)S(1)} custom-call(s32[256]{0:T(256)S(1)} %copy-done.1, f32[129,32,128]{2,1,0:T(8,128)S(1)} %bitcast.11), custom_call_target="tpu_custom_call" | custom-call | tf_op jit(solution)/shard_map/hand/pallas_call | solution.py:437
  136.2 1.8 %copy.13 = f32[256,27,128]{2,0,1:T(8,128)} copy(f32[256,27,128]{2,0,1:T(8,128)S(1)} %bitcast.10) | data formatting | bytes 7077888
  (1 shorter events, 0.0 us)
Async XLA Ops:
  47.7 1.6 %copy-start = (f32[4128,128]{1,0:T(8,128)S(1)}, f32[4128,128]{1,0:T(8,128)}, u32[]{:S(2)}) copy-start(f32[4128,128]{1,0:T(8,128)} %stencil.1) | copy-start | bytes 6340612
  49.3 0.7 copy-start.1
where the time goes:
time: 138 us
  Pallas kernels  129 us (93%)
  local copies, waits for them, and re-layouts  7.46 us (5%)
  other arithmetic  1.5 us (1%)
    pallas_call x1, Pallas kernels, per_device(): pl.pallas_call(functools.partial(hand_kernel, lax.axis_size('gx'), size),...  86.2 us
    pallas_call x1, Pallas kernels, per_device(): pl.pallas_call(compute_kernel, out_shape=jax.ShapeDtypeStruct(((columns +...  35.1 us
    pallas_call x1, Pallas kernels, per_device(): pl.pallas_call(functools.partial(halo_kernel, lax.axis_size('gx'), size),...  7.69 us
    unnamed x6, local copies, waits for them, and re-layouts  5.45 us

commit v1 on v0

v1 whole, which is shorter than its diff:
```python
import functools

import jax
import jax.numpy as jnp
import numpy as np
from jax import lax
from jax.experimental import pallas as pl
from jax.experimental.pallas import tpu as pltpu
from jax.sharding import PartitionSpec as P

CORNERS = [(a, b, c) for a in (0, 1) for b in (0, 1) for c in (0, 1)]
OFFSETS = [(a, b, c) for a in (-1, 0, 1) for b in (-1, 0, 1) for c in (-1, 0, 1)]
PAIRS = [(s, t) for s in range(8) for t in range(s, 8)]
PAIR_ROW = {pair: row for row, pair in enumerate(PAIRS)}
POINT_ROWS = 68
FACE_ROWS = 20


def corner_row(corner):
    return corner[0] * 4 + corner[1] * 2 + corner[2]


def point_row(offset):
    return (offset[0] + 1) * 9 + (offset[1] + 1) * 3 + offset[2] + 1


def pair_row(first, second):
    low, high = sorted((corner_row(first), corner_row(second)))
    return PAIR_ROW[low, high]


def edge_form(weight, root, store):
    def value(node, delta):
        offset = tuple(n - 2 * d for n, d in zip(node, delta))
        if min(offset) < -1 or max(offset) > 1:
            return None
        return weight(offset, delta)

    total = {}
    for direction in range(3):
        for node in CORNERS:
            other = tuple(n + (axis == direction) for axis, n in enumerate(node))
            face = root(node) * root(other)
            drops = []
            for delta in CORNERS:
                here, there = value(node, delta), value(other, delta)
                if here is None and there is None:
                    continue
                if there is None:
                    drops.append((delta, here))
                elif here is None:
                    drops.append((delta, -there))
                else:
                    drops.append((delta, here - there))
            for index, (first, drop) in enumerate(drops):
                scaled = face * drop
                for second, other_drop in drops[index:]:
                    row = pair_row(first, second)
                    term = scaled * other_drop
                    total[row] = total[row] + term if row in total else term
    for row, entry in total.items():
        store(row, entry)


SPLITS = (5, 11, 19)


def stencil_kernel(n_gx, n_gy, *refs):
    far, rest = refs[:9], refs[9:]
    out, rest = rest[0], rest[1:]
    low_x, high_x, low_y, high_y, edges, kbuf, logs, roots, wbuf, pairs, blocks, held = rest[:12]
    w_first, w_half, biases, onehot = rest[12:16]
    near = rest[16:25]
    own, owner, pick, w_in, w_mid, w_out, b_in, b_mid, b_out = near
    row_sems, halo_send, halo_recv, send_sems, recv_sems, own_sems = rest[25:]

    _, cx, cy, cz = own.shape
    nx, ny = cx + 4, cy + 4
    wide = cy + 2
    columns = cx * cy
    layers = w_mid.shape[0]
    devices = n_gx * n_gy
    by_point = out.shape[0] == 27
    slots = out.shape[1 if by_point else 0]
    most = slots // devices
    ix, iy = lax.axis_index("gx"), lax.axis_index("gy")
    me = ix * n_gy + iy
    mesh_id = pl.DeviceIdType.MESH
    half = n_gy // 2

    def partner(k):
        across = k // (devices // 2)
        side = (iy // half + 1 + across) % 2
        step = k % (devices // 2)
        return (ix + step % n_gx) % n_gx, side * half + (iy + step // n_gx) % half

    def each(action):
        pl.loop(0, devices // 2)(action)
        pl.loop(devices // 2 + 1, devices)(action)

    barrier = pltpu.get_barrier_semaphore()

    @each
    def _(k):
        px, py = partner(k)
        pl.semaphore_signal(barrier, inc=1, device_id=(px, py), device_id_type=mesh_id)

    fetches = [
        pltpu.make_async_copy(source, target, row_sems.at[number])
        for number, (source, target) in enumerate(zip(far, near))
    ]
    for fetch in fetches:
        fetch.start()

    ways = [(a, b) for a in (-1, 0, 1) for b in (-1, 0, 1) if a or b]

    def exists(way):
        x, y = ix + way[0], iy + way[1]
        return (x >= 0) & (x < n_gx) & (y >= 0) & (y < n_gy)

    def landing(way):
        if way[1] == 0:
            return low_x if way[0] < 0 else high_x
        rim = low_y if way[1] < 0 else high_y
        start = (0, 2, cx + 2)[way[0] + 1]
        return rim.at[:, pl.ds(start, cx if way[0] == 0 else 2)]

    def leaving(way):
        if way[1] == 0:
            return own.at[:, pl.ds(0 if way[0] < 0 else cx - 2, 2)]
        rim = edges.at[0 if way[1] < 0 else 1]
        return rim.at[:, pl.ds(cx - 2 if way[0] > 0 else 0, cx if way[0] == 0 else 2)]

    def halo(number, way):
        return pltpu.make_async_remote_copy(
            src_ref=leaving(way),
            dst_ref=landing((-way[0], -way[1])),
            send_sem=halo_send.at[number],
            recv_sem=halo_recv.at[number],
            device_id=(ix + way[0], iy + way[1]),
            device_id_type=mesh_id,
        )

    for way in ways:
        @pl.when(jnp.logical_not(exists(way)))
        def _(way=way):
            part = landing(way)
            part[...] = jnp.zeros(part.shape, jnp.float32)

    fetches[0].wait()
    edges[0] = own[:, :, :2, :]
    edges[1] = own[:, :, cy - 2:, :]

    lane = lax.broadcasted_iota(jnp.int32, (8, cz), 1)

    def log_rows(x, y):
        kappa = kbuf[pl.ds(pl.multiple_of((x * ny + y) * 8, 8), 8), :]
        value = jnp.log1p(kappa)
        below = jnp.where(lane == 0, 0.0, pltpu.roll(value, 1, 1))
        logs[x * ny + y] = jnp.concatenate([value, below], axis=0).astype(jnp.bfloat16)

    for p in range(8):
        for x in range(2, cx + 2):
            kbuf[pl.ds((x * ny + 2) * 8 + p, cy, stride=8), :] = own[p, x - 2]

    @pl.loop(2, cx + 2)
    def _(x):
        for y in range(2, cy + 2):
            log_rows(x, y)

    pl.semaphore_wait(barrier, devices - 1)
    for number, way in enumerate(ways):
        @pl.when(exists(way))
        def _(number=number, way=way):
            halo(number, way).start()

    for fetch in fetches[1:]:
        fetch.wait()
    w_first[...] = (0.5 * lax.dot_general(
        w_in[...], pick[...], (((0,), (0,)), ((), ())), preferred_element_type=jnp.float32
    )).astype(jnp.bfloat16)
    for m in range(layers):
        w_half[m] = w_mid[m] * jnp.bfloat16(0.5)
    w_half[layers] = jnp.zeros(w_half.shape[1:], jnp.bfloat16)
    w_half[layers, :27] = w_out[...] * jnp.bfloat16(0.5)
    for m in range(layers + 2):
        if m > layers:
            bias = b_out[...]
            rows = 32
            bias = jnp.concatenate([bias, jnp.zeros((1, cz - 27), jnp.float32)], axis=1)
        else:
            bias = b_in[...] if m == 0 else b_mid[m - 1:m, :]
        biases[m] = jnp.transpose(jnp.broadcast_to(0.5 * bias, biases.shape[1:]))

    spread = lax.broadcasted_iota(jnp.int32, (cy, columns), 1) % cy == lax.broadcasted_iota(
        jnp.int32, (cy, columns), 0
    )
    tiled = jnp.dot(
        owner[...].astype(jnp.float32).astype(jnp.bfloat16),
        jnp.where(spread, 1.0, 0.0).astype(jnp.bfloat16),
        preferred_element_type=jnp.float32,
    )
    mine_row = lax.broadcasted_iota(jnp.int32, (cx, columns), 1) // cy == lax.broadcasted_iota(
        jnp.int32, (cx, columns), 0
    )
    owners = jnp.sum(jnp.where(mine_row, tiled, 0.0), axis=0, keepdims=True)
    across = jnp.broadcast_to(owners, (columns, columns))
    earlier = lax.broadcasted_iota(jnp.int32, (columns, columns), 0) < lax.broadcasted_iota(
        jnp.int32, (columns, columns), 1
    )
    same = (across == jnp.transpose(across)) & earlier
    rank = jnp.sum(jnp.where(same, 1.0, 0.0), axis=0, keepdims=True)
    slot = owners * most + rank
    number = lax.broadcasted_iota(jnp.int32, (slots, columns), 0).astype(jnp.float32)
    hit = jnp.where(number == slot, 1.0, 0.0).astype(jnp.bfloat16)
    for third in range(3):
        onehot[:, third * columns:(third + 1) * columns] = hit

    total = (cx + 2) * wide
    group = max(g for g in range(1, 7) if total % g == 0)
    inner = (cx - 1) * (cy - 1)
    lane_out = lax.broadcasted_iota(jnp.int32, (32, cz), 1)

    def place(i):
        j = i - inner
        q = j - 3 * wide
        s, t = j // wide, q % 3
        x = jnp.where(
            q >= 0, 3 + q // 3,
            jnp.where(j >= 0, 1 + s + (cx - 1) * (s // 2), 3 + i // (cy - 1)),
        )
        y = jnp.where(
            q >= 0, 1 + t + (cy - 1) * (t // 2),
            jnp.where(j >= 0, 1 + j % wide, 3 + i % (cy - 1)),
        )
        return x, y

    def activate(value):
        return (value + value * jnp.tanh(value)).astype(jnp.bfloat16)

    def biased(value, m):
        bias = biases[m, :value.shape[0], :]
        return value + jnp.concatenate([bias] * group, axis=1)

    def predict(step):
        places = [place(step * group + k) for k in range(group)]
        parts = []
        for x, y in places:
            at = x * ny + y
            parts.append(
                jnp.concatenate([logs[at], logs[at - ny], logs[at - 1], logs[at - ny - 1]], axis=0)
            )
        rows = jnp.concatenate(parts, axis=1)
        hidden = activate(biased(jnp.dot(w_first[...], rows, preferred_element_type=jnp.float32), 0))
        for m in range(layers):
            hidden = activate(
                biased(jnp.dot(w_half[m], hidden, preferred_element_type=jnp.float32), m + 1)
            )
        last = jnp.dot(w_half[layers, :32], hidden, preferred_element_type=jnp.float32)
        weights = 0.25 + 0.25 * jnp.tanh(biased(last, layers + 1))
        for k, (x, y) in enumerate(places):
            outside = (
                ((x == 1) & (ix == 0))
                | ((x == cx + 2) & (ix == n_gx - 1))
                | ((y == 1) & (iy == 0))
                | ((y == cy + 2) & (iy == n_gy - 1))
            )
            keep = jnp.where(outside, 0.0, 1.0)
            column = weights[:, k * cz:(k + 1) * cz] * keep
            above = jnp.where(lane_out == cz - 1, 0.0, pltpu.roll(column, cz - 1, 1))
            row = ((x - 1) * wide + y - 1) * POINT_ROWS
            wbuf[pl.ds(row, 32), :] = column
            wbuf[pl.ds(row + 32, 32), :] = above

    pl.loop(0, inner // group)(predict)

    for number, way in enumerate(ways):
        @pl.when(exists(way))
        def _(number=number, way=way):
            halo(number, way).wait_send()

        @pl.when(exists((-way[0], -way[1])))
        def _(number=number, way=way):
            halo(number, way).wait_recv()

    for p in range(8):
        for x in range(nx):
            start = x * ny * 8 + p
            if x < 2 or x >= cx + 2:
                middle = low_x[p, x] if x < 2 else high_x[p, x - 2 - cx]
                kbuf[pl.ds(start + 16, cy, stride=8), :] = middle
            kbuf[pl.ds(start, 2, stride=8), :] = low_y[p, x]
            kbuf[pl.ds(start + (cy + 2) * 8, 2, stride=8), :] = high_y[p, x]

    @pl.loop(0, 4)
    def _(s):
        x = s + cx * (s // 2)
        for y in range(ny):
            log_rows(x, y)

    @pl.loop(2, cx + 2)
    def _(x):
        for y in (0, 1, cy + 2, cy + 3):
            log_rows(x, y)

    @pl.loop(1, nx - 1)
    def _(x):
        for y in range(1, ny - 1):
            root = jnp.sqrt(kbuf[pl.ds(pl.multiple_of((x * ny + y) * 8, 8), 8), :])
            above = jnp.where(lane == cz - 1, 0.0, pltpu.roll(root, cz - 1, 1))
            row = ((x - 1) * wide + y - 1) * FACE_ROWS
            roots[pl.ds(row, 8), :] = root
            roots[pl.ds(row + 8, 8), :] = above

    pl.loop(inner // group, total // group)(predict)

    @pl.loop(0, pl.cdiv((cx + 1) * wide, 8))
    def _(tile):
        base = tile * 8

        def weight(offset, delta):
            column = base + delta[0] * wide + delta[1]
            row = point_row(offset) + 32 * delta[2]
            return wbuf[pl.ds(column * POINT_ROWS + row, 8, stride=POINT_ROWS), :]

        def root(node):
            column = base + node[0] // 2 * wide + node[1] // 2
            row = corner_row(tuple(n % 2 for n in node)) + 8 * (node[2] // 2)
            return roots[pl.ds(column * FACE_ROWS + row, 8, stride=FACE_ROWS), :]

        def store(row, entry):
            pairs[pl.ds(base * len(PAIRS) + row, 8, stride=len(PAIRS)), :] = entry

        edge_form(weight, root, store)

    def lay(first_row, last_row):
        @pl.loop(0, cx * (cy // 8))
        def _(tile):
            x = tile // (cy // 8)
            y = tile % (cy // 8) * 8
            cell = (x + 1) * wide + y + 1
            for number in range(first_row, last_row):
                offset = OFFSETS[number]
                sums = [None, None]
                for first in CORNERS:
                    second = tuple(f + o for f, o in zip(first, offset))
                    if min(second) < 0 or max(second) > 1:
                        continue
                    base = cell - first[0] * wide - first[1]
                    start = base * len(PAIRS) + pair_row(first, second)
                    entry = pairs[pl.ds(start, 8, stride=len(PAIRS)), :]
                    seen = sums[first[2]]
                    sums[first[2]] = entry if seen is None else seen + entry
                if sums[1] is not None:
                    moved = pltpu.roll(sums[1], 1, 1)
                    sums[0] = moved if sums[0] is None else sums[0] + moved
                blocks[number, pl.ds(pl.multiple_of(x * cy + y, 8), 8), :] = sums[0]

        @pl.loop(first_row, last_row)
        def _(number):
            block = blocks[number]
            top = block.astype(jnp.bfloat16)
            left = block - top.astype(jnp.float32)
            middle = left.astype(jnp.bfloat16)
            bottom = (left - middle.astype(jnp.float32)).astype(jnp.bfloat16)
            placed = jnp.dot(
                onehot[...],
                jnp.concatenate([top, middle, bottom], axis=0),
                preferred_element_type=jnp.float32,
            )
            if by_point:
                held[number] = placed
            else:
                held[:, number, :] = placed

    bounds = (0, *SPLITS, 27) if by_point else (0, 27)

    def slots_of(ref, part, device):
        if by_point:
            rows = pl.ds(bounds[part], bounds[part + 1] - bounds[part])
            return ref.at[rows, pl.ds(pl.multiple_of(device * most, 8), most)]
        return ref.at[pl.ds(device * most, most)]

    def copy(part, k, home):
        px, py = partner(k)
        other = px * n_gy + py
        return pltpu.make_async_remote_copy(
            src_ref=slots_of(held, part, other),
            dst_ref=slots_of(out, part, home),
            send_sem=send_sems.at[part, other],
            recv_sem=recv_sems.at[part, home],
            device_id=(px, py),
            device_id_type=mesh_id,
        )

    def stay(part):
        return pltpu.make_async_copy(
            slots_of(held, part, me), slots_of(out, part, me), own_sems.at[part]
        )

    for part in range(len(bounds) - 1):
        lay(bounds[part], bounds[part + 1])

        @each
        def _(k, part=part):
            copy(part, k, me).start()

        stay(part).start()

    for part in range(len(bounds) - 1):
        @each
        def _(k, part=part):
            px, py = partner(k)
            copy(part, k, me).wait_send()
            copy(part, k, px * n_gy + py).wait_recv()

        stay(part).wait()


def per_device(coefficient, owner, w_in, b_in, w_mid, b_mid, w_out, b_out):
    cx, cy, cz = coefficient.shape[3:]
    hid = w_in.shape[0]
    n_gx, n_gy = lax.axis_size("gx"), lax.axis_size("gy")
    devices = n_gx * n_gy
    columns = cx * cy
    most = 2 * columns // devices
    slots = devices * most

    pick = np.zeros((27, 64), np.float32)
    row = 0
    for dx, dy in ((0, 0), (1, 0), (0, 1), (1, 1)):
        for dz in (0, 1):
            for corner in CORNERS:
                shift = (dx, dy, dz)
                if all(s <= c for s, c in zip(shift, corner)):
                    pick[point_row(tuple(c - 2 * s for s, c in zip(shift, corner))), row] = 1.0
                row += 1

    wide = cy + 2
    tiles = -(-((cx + 1) * wide) // 8) * 8
    spread = max((cx + 2) * wide, tiles + wide + 2)
    small = (
        coefficient.reshape(8, cx, cy, cz), owner, jnp.asarray(pick, jnp.bfloat16),
        w_in.T, w_mid, w_out, b_in[None, :], b_mid, b_out[None, :],
    )
    by_point = most % 8 == 0
    shape = (27, slots, cz) if by_point else (slots, 27, cz)
    parts = len(SPLITS) + 1 if by_point else 1
    f32, bf16 = jnp.float32, jnp.bfloat16
    relaid = pl.pallas_call(
        functools.partial(stencil_kernel, n_gx, n_gy),
        out_shape=jax.ShapeDtypeStruct(shape, f32),
        in_specs=[pl.BlockSpec(memory_space=pltpu.HBM)] * len(small),
        out_specs=pl.BlockSpec(memory_space=pl.ANY),
        scratch_shapes=[
            pltpu.VMEM((8, 2, cy, cz), f32),
            pltpu.VMEM((8, 2, cy, cz), f32),
            pltpu.VMEM((8, cx + 4, 2, cz), f32),
            pltpu.VMEM((8, cx + 4, 2, cz), f32),
            pltpu.VMEM((2, 8, cx, 2, cz), f32),
            pltpu.VMEM(((cx + 4) * (cy + 4) * 8 + 8, cz), f32),
            pltpu.VMEM(((cx + 4) * (cy + 4), 16, cz), bf16),
            pltpu.VMEM(((spread + 1) * FACE_ROWS, cz), f32),
            pltpu.VMEM(((spread + 1) * POINT_ROWS, cz), f32),
            pltpu.VMEM(((tiles + 1) * len(PAIRS), cz), f32),
            pltpu.VMEM((27, columns, cz), f32),
            pltpu.VMEM(shape, f32),
            pltpu.VMEM((hid, 64), bf16),
            pltpu.VMEM((w_mid.shape[0] + 1, hid, hid), bf16),
            pltpu.VMEM((w_mid.shape[0] + 2, hid, cz), f32),
            pltpu.VMEM((slots, 3 * columns), bf16),
            *[pltpu.VMEM(part.shape, part.dtype) for part in small],
            pltpu.SemaphoreType.DMA((len(small),)),
            pltpu.SemaphoreType.DMA((8,)),
            pltpu.SemaphoreType.DMA((8,)),
            pltpu.SemaphoreType.DMA((parts, devices)),
            pltpu.SemaphoreType.DMA((parts, devices)),
            pltpu.SemaphoreType.DMA((parts,)),
        ],
        compiler_params=pltpu.CompilerParams(
            collective_id=0, has_side_effects=True, vmem_limit_bytes=60 << 20
        ),
        name="stencil",
    )(*small)
    return jnp.transpose(relaid, (1, 0, 2)) if by_point else relaid


def solution(mesh):
    return jax.shard_map(
        per_device,
        mesh=mesh,
        in_specs=(
            P(None, None, None, "gx", "gy", None),
            P("gx", "gy"),
            P(),
            P(),
            P(),
            P(),
            P(),
            P(),
        ),
        out_specs=P(("gx", "gy"), None, None),
        check_vma=False,
    )
```

time: 138 us -> 124 us (0.90)
  Pallas kernels: 129 us -> 119 us
  local copies, waits for them, and re-layouts: 7.46 us -> 4.17 us
  other arithmetic: 1.5 us -> 0 us
    pallas_call x3 -> x1, Pallas kernels: 129 us -> 119 us  [per_device(): pl.pallas_call(functools.partial(stencil_kernel, n_gx, n_gy), out_shape=j...]
    unnamed x6 -> x1, local copies, waits for them, and re-layouts: 5.45 us -> 4.17 us
where the time goes in v1:
time: 124 us
  Pallas kernels  119 us (96%)
  local copies, waits for them, and re-layouts  4.17 us (3%)
    pallas_call x1, Pallas kernels, per_device(): pl.pallas_call(functools.partial(stencil_kernel, n_gx, n_gy), out_shape=j...  119 us
    unnamed x1, local copies, waits for them, and re-layouts  4.17 us

profile of v1, /device:TPU:8, one launch (start us, length us, event | category | flops | bytes accessed | tf_op | source)
XLA Modules:
  0.0 123.6 jit_solution(9152075352989260746)
XLA Ops:
  0.0 119.4 %stencil.1 = f32[27,256,128]{2,1,0:T(8,128)} custom-call(f32[8,8,16,128]{3,2,1,0:T(8,128)} %bitcast.6, s32[8,16]{1,0:T(8,128)} %refs_1_.1, bf16[27,64]{1,0:T(8,128)(2,1)} %constant.2.clone.refs_2_, bf16[27,128]{1,0:T(8,128)(2,1)} %bitcast.7, bf16[2,128,128]{2,1,0:T(8,128)(2,1)} %refs_4_.1, bf16[27,128]{1,0:T(8,128)(2,1)} %refs_5_.1, f32[1,128]{1,0:T(1,128)} %bitcast.8, ...), custom_call_target="tpu_custom_call" | custom-call | tf_op jit(solution)/shard_map/stencil/pallas_call | solution.py:450
  119.4 4.2 %copy.11 = f32[256,27,128]{2,0,1:T(8,128)} copy(f32[256,27,128]{2,0,1:T(8,128)} %bitcast.5) | data formatting | bytes 7077888

commit v2 on v1

--- a/solution.py
+++ b/solution.py
@@ -71,8 +71,10 @@
     low_x, high_x, low_y, high_y, edges, kbuf, logs, roots, wbuf, pairs, blocks, held = rest[:12]
     w_first, w_half, biases, onehot = rest[12:16]
     near = rest[16:25]
+    stages = rest[25:25 + near[4].shape[0] + 1]
+    rest = rest[25 + len(stages):]
     own, owner, pick, w_in, w_mid, w_out, b_in, b_mid, b_out = near
-    row_sems, halo_send, halo_recv, send_sems, recv_sems, own_sems = rest[25:]
+    row_sems, halo_send, halo_recv, send_sems, recv_sems, own_sems = rest
 
     _, cx, cy, cz = own.shape
     nx, ny = cx + 4, cy + 4
@@ -221,19 +223,33 @@
     inner = (cx - 1) * (cy - 1)
     lane_out = lax.broadcasted_iota(jnp.int32, (32, cz), 1)
 
-    def place(i):
-        j = i - inner
-        q = j - 3 * wide
-        s, t = j // wide, q % 3
-        x = jnp.where(
-            q >= 0, 3 + q // 3,
-            jnp.where(j >= 0, 1 + s + (cx - 1) * (s // 2), 3 + i // (cy - 1)),
-        )
-        y = jnp.where(
-            q >= 0, 1 + t + (cy - 1) * (t // 2),
-            jnp.where(j >= 0, 1 + j % wide, 3 + i % (cy - 1)),
-        )
-        return x, y
+    bands = inner // group
+    period = 2 * (cy - 1) // group
+    turn = (cx - 1) * wide // group
+    lines = wide // group
+    assert period * group == 2 * (cy - 1) and turn * group == (cx - 1) * wide
+    assert lines * group == wide and group % 3 == 0
+
+    def places(step):
+        block = step // period
+        start = (step - block * period) * group
+        rim = step - turn
+        line = rim // lines
+        rim_x = 1 + line + (cx - 1) * (line // 2)
+        rim_y = 1 + (rim - line * lines) * group
+        found = []
+        for k in range(group):
+            at = start + k
+            second = (at >= cy - 1).astype(jnp.int32)
+            x, y = 3 + 2 * block + second, 3 + at - (cy - 1) * second
+            behind = inner % group
+            t = (k - behind) % 3
+            side = step >= bands + (0 if k >= behind else 1)
+            side_x = 3 + (group // 3) * (step - bands) + (k - behind) // 3
+            x = jnp.where(side, side_x, x)
+            y = jnp.where(side, 1 + t + (cy - 1) * (t // 2), y)
+            found.append((jnp.where(rim >= 0, rim_x, x), jnp.where(rim >= 0, rim_y + k, y)))
+        return found
 
     def activate(value):
         return (value + value * jnp.tanh(value)).astype(jnp.bfloat16)
@@ -242,23 +258,14 @@
         bias = biases[m, :value.shape[0], :]
         return value + jnp.concatenate([bias] * group, axis=1)
 
-    def predict(step):
-        places = [place(step * group + k) for k in range(group)]
-        parts = []
-        for x, y in places:
-            at = x * ny + y
-            parts.append(
-                jnp.concatenate([logs[at], logs[at - ny], logs[at - 1], logs[at - ny - 1]], axis=0)
-            )
-        rows = jnp.concatenate(parts, axis=1)
-        hidden = activate(biased(jnp.dot(w_first[...], rows, preferred_element_type=jnp.float32), 0))
-        for m in range(layers):
-            hidden = activate(
-                biased(jnp.dot(w_half[m], hidden, preferred_element_type=jnp.float32), m + 1)
-            )
-        last = jnp.dot(w_half[layers, :32], hidden, preferred_element_type=jnp.float32)
+    steps = total // group
+
+    def predict(tick):
+        hidden = stages[layers]
+        last = jnp.dot(w_half[layers, :32], hidden[...], preferred_element_type=jnp.float32)
         weights = 0.25 + 0.25 * jnp.tanh(biased(last, layers + 1))
-        for k, (x, y) in enumerate(places):
+        done = jnp.maximum(tick - layers - 1, 0)
+        for k, (x, y) in enumerate(places(done)):
             outside = (
                 ((x == 1) & (ix == 0))
                 | ((x == cx + 2) & (ix == n_gx - 1))
@@ -271,6 +278,24 @@
             row = ((x - 1) * wide + y - 1) * POINT_ROWS
             wbuf[pl.ds(row, 32), :] = column
             wbuf[pl.ds(row + 32, 32), :] = above
+        for m in reversed(range(layers)):
+            stages[m + 1][...] = activate(
+                biased(jnp.dot(w_half[m], stages[m][...], preferred_element_type=jnp.float32), m + 1)
+            )
+        fresh = jnp.minimum(tick, steps - 1)
+        parts = []
+        for x, y in places(fresh):
+            at = x * ny + y
+            parts.append(
+                jnp.concatenate([logs[at], logs[at - ny], logs[at - 1], logs[at - ny - 1]], axis=0)
+            )
+        rows = jnp.concatenate(parts, axis=1)
+        stages[0][...] = activate(
+            biased(jnp.dot(w_first[...], rows, preferred_element_type=jnp.float32), 0)
+        )
+
+    for stage in stages:
+        stage[...] = jnp.zeros(stage.shape, stage.dtype)
 
     pl.loop(0, inner // group)(predict)
 
@@ -312,7 +337,7 @@
             roots[pl.ds(row, 8), :] = root
             roots[pl.ds(row + 8, 8), :] = above
 
-    pl.loop(inner // group, total // group)(predict)
+    pl.loop(inner // group, steps + layers + 1)(predict)
 
     @pl.loop(0, pl.cdiv((cx + 1) * wide, 8))
     def _(tile):
@@ -443,6 +468,7 @@
         coefficient.reshape(8, cx, cy, cz), owner, jnp.asarray(pick, jnp.bfloat16),
         w_in.T, w_mid, w_out, b_in[None, :], b_mid, b_out[None, :],
     )
+    group = max(g for g in range(1, 7) if (cx + 2) * wide % g == 0)
     by_point = most % 8 == 0
     shape = (27, slots, cz) if by_point else (slots, 27, cz)
     parts = len(SPLITS) + 1 if by_point else 1
@@ -470,6 +496,7 @@
             pltpu.VMEM((w_mid.shape[0] + 2, hid, cz), f32),
             pltpu.VMEM((slots, 3 * columns), bf16),
             *[pltpu.VMEM(part.shape, part.dtype) for part in small],
+            *[pltpu.VMEM((hid, group * cz), bf16)] * (w_mid.shape[0] + 1),
             pltpu.SemaphoreType.DMA((len(small),)),
             pltpu.SemaphoreType.DMA((8,)),
             pltpu.SemaphoreType.DMA((8,)),
@@ -478,7 +505,7 @@
             pltpu.SemaphoreType.DMA((parts,)),
         ],
         compiler_params=pltpu.CompilerParams(
-            collective_id=0, has_side_effects=True, vmem_limit_bytes=60 << 20
+            collective_id=0, has_side_effects=True, vmem_limit_bytes=28 << 20
         ),
         name="stencil",
     )(*small)

time: 124 us -> 114 us (0.919)
  Pallas kernels: 119 us -> 105 us
  local copies, waits for them, and re-layouts: 4.17 us -> 8.44 us
    pallas_call x1, Pallas kernels: 119 us -> 105 us  [per_device(): pl.pallas_call(functools.partial(stencil_kernel, n_gx, n_gy), out_shape=j...]
    unnamed x1 -> x19, local copies, waits for them, and re-layouts: 4.17 us -> 8.44 us
where the time goes in v2:
time: 114 us
  Pallas kernels  105 us (92%)
  local copies, waits for them, and re-layouts  8.44 us (7%)
    pallas_call x1, Pallas kernels, per_device(): pl.pallas_call(functools.partial(stencil_kernel, n_gx, n_gy), out_shape=j...  105 us
    unnamed x19, local copies, waits for them, and re-layouts  8.44 us

profile of v2, /device:TPU:8, one launch (start us, length us, event | category | flops | bytes accessed | tf_op | source)
XLA Modules:
  0.0 113.6 jit_solution(16761252831859394697)
XLA Ops:
  0.0 0.0 copy-start
  0.0 1.0 copy-done
  1.0 0.0 copy-start.1
  1.0 0.8 copy-done.1
  1.9 0.0 copy-start.2
  1.9 0.7 copy-done.2
  2.6 0.0 copy-start.3
  2.6 0.7 copy-done.3
  3.3 0.0 copy-start.4
  3.3 0.7 copy-done.4
  4.0 0.0 copy-start.5
  4.0 0.7 copy-done.5
  4.7 0.0 copy-start.6
  4.7 0.7 copy-done.6
  5.3 0.0 copy-start.7
  5.3 0.7 copy-done.7
  6.0 0.0 copy-start.8
  6.0 0.7 copy-done.8
  6.7 105.1 %stencil.1 = f32[27,256,128]{2,1,0:T(8,128)S(1)} custom-call(f32[8,8,16,128]{3,2,1,0:T(8,128)S(1)} %bitcast.6, s32[8,16]{1,0:T(8,128)S(1)} %copy-done.5, bf16[27,64]{1,0:T(8,128)(2,1)S(1)} %copy-done.4, bf16[27,128]{1,0:T(8,128)(2,1)S(1)} %bitcast.7, bf16[2,128,128]{2,1,0:T(8,128)(2,1)S(1)} %copy-done.1, bf16[27,128]{1,0:T(8,128)(2,1)S(1)} %copy-done.3, ...), custom_call_target="tpu_custom_call" | custom-call | tf_op jit(solution)/shard_map/stencil/pallas_call | solution.py:476
  111.8 1.8 %copy.11 = f32[256,27,128]{2,0,1:T(8,128)} copy(f32[256,27,128]{2,0,1:T(8,128)S(1)} %bitcast.5) | data formatting | bytes 7077888
Async XLA Ops:
  0.0 1.0 copy-start
  1.0 0.8 copy-start.1
  1.9 0.7 copy-start.2
  2.6 0.7 copy-start.3
  3.3 0.7 copy-start.4
  4.0 0.7 copy-start.5
  4.7 0.7 copy-start.6
  5.3 0.7 copy-start.7
  6.0 0.7 copy-start.8
